TPU v7x, 128 devices: a whole 4x4x4 slice. The times are simulated.
128 devices in a mesh: ex: 16 (over z, y), ey: 8 (over x, core).
Axes of the slice: x: 4, y: 4, z: 4, core: 2. Of those that a mesh axis runs over, the one named last changes fastest.
Arguments:
- tokens: bfloat16 [32768, 768], P(('ex', 'ey')), may hold values from -6 to 6
- routes: int32 [32768, 1], P(('ex', 'ey')), may hold values from 0 to 127; in each aligned block of 256 rows (0 to 255, 256 to 511, ...) at most 4 rows name the same one
- sub_expert: int32 [32768], P(('ex', 'ey')), may hold values from 0 to 1
- probability: float32 [32768], P(('ex', 'ey')), may hold values from 0.2 to 1
- weight_in: bfloat16 [256, 768, 3072], P(('ex', 'ey')), may hold values from -0.21875 to 0.21875
- weight_out: bfloat16 [256, 3072, 768], P(('ex', 'ey')), may hold values from -0.109375 to 0.109375
Outputs:
- mixed: bfloat16 [32768, 768], P(('ex', 'ey'))
Inputs may be any that keep to these rules, and one draw needn't show every extreme that they name: `routes`: among the 256 tokens of one device (aligned blocks of rows), no value is named by more than 4 tokens, a bound that some block reaches.
All inputs are finite; a program needn't handle non-finite values.
Results may differ from a plain program's by a relative error of at most 0.0058.
Values may be sent and summed in bfloat16 or wider, within the bound.
A program may use at most 64 MiB of HBM per device.

v0:
```python
import jax
import jax.numpy as jnp
from jax import lax
from jax.sharding import PartitionSpec as P


def local(tokens, routes, sub_expert, probability, weight_in, weight_out):
    count_ex = lax.axis_size("ex")
    count_ey = lax.axis_size("ey")
    devices_all = count_ex * count_ey
    local_experts = weight_in.shape[0]
    tok_rows = tokens.shape[0]
    width = tokens.shape[1]
    capacity = 2 * tok_rows // devices_all
    owner = routes[:, 0]
    label_key = owner * local_experts + sub_expert
    groups = local_experts * devices_all
    onehot = (label_key[:, None] == jnp.arange(groups, dtype=jnp.int32)[None, :]).astype(
        jnp.bfloat16
    )
    positions = jnp.arange(tok_rows, dtype=jnp.int32)
    earlier = (positions[:, None] > positions[None, :]).astype(jnp.bfloat16)
    before = jnp.dot(earlier, onehot, preferred_element_type=jnp.float32)
    slot = jnp.sum(before * onehot.astype(jnp.float32), axis=1).astype(jnp.int32)
    target = sub_expert * (devices_all * capacity) + owner * capacity + slot
    buffer_rows = jnp.arange(groups * capacity, dtype=jnp.int32)
    placing = (buffer_rows[:, None] == target[None, :]).astype(jnp.bfloat16)
    outgoing = jnp.dot(placing, tokens, preferred_element_type=jnp.float32).astype(jnp.bfloat16)
    arrive_rows = devices_all * capacity
    labels = jnp.full((groups * capacity,), local_experts, jnp.int32).at[target].set(sub_expert)
    shaped = outgoing.reshape(local_experts, devices_all, capacity, width)
    label_shaped = labels.reshape(local_experts, devices_all, capacity)
    arrived, labels_in = (
        lax.all_to_all(shaped, ("ex", "ey"), split_axis=1, concat_axis=1, tiled=True),
        lax.all_to_all(label_shaped, ("ex", "ey"), split_axis=1, concat_axis=1, tiled=True),
    )
    batch = arrived.reshape(local_experts, arrive_rows, width)
    hidden = jax.nn.relu(
        jnp.einsum("lrd,ldf->lrf", batch, weight_in, preferred_element_type=jnp.float32)
    ).astype(jnp.bfloat16)
    result = jnp.einsum(
        "lrf,lfd->lrd", hidden, weight_out, preferred_element_type=jnp.float32
    ).astype(jnp.bfloat16)
    shaped_back = result.reshape(local_experts, devices_all, capacity, width)
    returned = lax.all_to_all(shaped_back, ("ex", "ey"), split_axis=1, concat_axis=1, tiled=True)
    back_rows = returned.reshape(groups * capacity, width)
    gathered = jnp.einsum("rt,rd->td", placing, back_rows, preferred_element_type=jnp.float32)
    return (gathered * probability[:, None]).astype(jnp.bfloat16)


def solution(mesh):
    return jax.shard_map(
        local,
        mesh=mesh,
        in_specs=(
            P(("ex", "ey"), None),
            P(("ex", "ey"), None),
            P(("ex", "ey")),
            P(("ex", "ey")),
            P(("ex", "ey"), None, None),
            P(("ex", "ey"), None, None),
        ),
        out_specs=P(("ex", "ey"), None),
        check_vma=False,
    )
```

profile of v0, /device:TPU:1, one launch (start us, length us, event | category | flops | bytes accessed | tf_op | source)
XLA Modules:
  0.0 84.4 jit_solution(5231021807757352854)
XLA Ops:
  0.0 0.0 copy-start
  0.0 0.7 broadcast_multiply_fusion.1
  0.7 0.7 add.10
  1.4 0.3 fusion.2
  1.7 0.7 convert_add_fusion
  2.4 0.0 copy-done
  2.4 0.6 convolution_convert_fusion.1
  3.0 0.4 reshape.19
  3.4 0.0 copy-start.1
  3.4 0.5 copy.9
  3.9 36.2 %all_to_all.10 = bf16[2,128,4,768]{3,2,0,1:T(4,128)(2,1)S(1)} all-to-all(bf16[2,128,4,768]{3,2,0,1:T(4,128)(2,1)S(1)} %copy.9), channel_id=1, replica_groups=mesh['ex'=16,'ey'=8] {'ex','ey'}, dimensions={1} | all-to-all | bytes 3145728 | tf_op jit(solution)/shard_map/all_to_all | solution.py:34
  40.2 0.0 slice-start
  40.2 1.2 %copy.10 = bf16[2,128,4,768]{3,0,2,1:T(2,128)(2,1)S(1)} copy(bf16[2,128,4,768]{3,2,0,1:T(4,128)(2,1)S(1)} %all_to_all.10) | data formatting | bytes 3145728 | tf_op jit(solution)/shard_map/all_to_all | solution.py:34
  41.4 0.0 copy-done.1
  41.4 0.0 slice-start.1
  41.4 0.0 slice-start.2
  41.4 5.3 %maximum_convert_fusion = bf16[2,512,3072]{2,1,0:T(8,128)(2,1)S(1)} fusion(bf16[2,768,3072]{2,1,0:T(8,128)(2,1)S(1)} %copy-done.1, bf16[2,512,768]{2,0,1:T(2,128)(2,1)S(1)} %bitcast.8), kind=kOutput, calls=%fused_computation | convolution fusion | flops 4838129664 | bytes 17301504 | tf_op jit(solution)/shard_map/lrd,ldf->lrf/dot_general | solution.py:39
  46.8 0.0 slice-done
  46.8 0.0 slice-done.1
  46.8 0.0 slice-done.2
  46.8 5.1 %convolution_convert_fusion = bf16[2,512,768]{2,1,0:T(8,128)(2,1)S(1)} fusion(bf16[2,512,3072]{2,1,0:T(8,128)(2,1)S(1)} %maximum_convert_fusion, bf16[2,3072,768]{2,1,0:T(8,128)(2,1)S(1)} %bitcast.12), kind=kOutput, calls=%fused_computation.1 | convolution fusion | flops 4832624640 | bytes 17301504 | tf_op jit(solution)/shard_map/lrf,lfd->lrd/dot_general | solution.py:41
  51.9 0.4 reshape.21
  52.3 0.5 copy.12
  52.9 28.9 %all_to_all.11 = bf16[2,128,4,768]{3,2,0,1:T(4,128)(2,1)S(1)} all-to-all(bf16[2,128,4,768]{3,2,0,1:T(4,128)(2,1)S(1)} %copy.12), channel_id=1, replica_groups=mesh['ex'=16,'ey'=8] {'ex','ey'}, dimensions={1} | all-to-all | bytes 3145728 | tf_op jit(solution)/shard_map/all_to_all | solution.py:45
  81.8 0.5 copy.13
  82.3 0.0 copy-start.2
  82.3 0.4 reshape.22
  82.7 0.3 copy-done.2
  83.0 1.4 %fusion.1 = bf16[256,768]{1,0:T(8,128)(2,1)} fusion(bf16[1024,768]{1,0:T(8,128)(2,1)S(1)} %reshape.22, s32[256]{0:T(256)S(1)} %convert_add_fusion, f32[256]{0:T(256)S(1)} %copy-done.2), kind=kOutput, calls=%fused_computation.5 | convolution fusion | flops 403308544 | bytes 1968128 | tf_op jit(solution)/shard_map/rt,rd->td/dot_general | solution.py:47
  (1 shorter events, 0.0 us)
Async XLA Ops:
  0.0 2.4 %copy-start = (bf16[256,768]{1,0:T(8,128)(2,1)S(1)}, bf16[256,768]{1,0:T(8,128)(2,1)}, u32[]{:S(2)}) copy-start(bf16[256,768]{1,0:T(8,128)(2,1)} %param.6) | copy-start | bytes 1179652
  3.4 38.0 %copy-start.1 = (bf16[2,768,3072]{2,1,0:T(8,128)(2,1)S(1)}, bf16[2,768,3072]{2,1,0:T(8,128)(2,1)}, u32[]{:S(2)}) copy-start(bf16[2,768,3072]{2,1,0:T(8,128)(2,1)} %param.10) | copy-start | bytes 28311556
  40.2 6.6 %slice-start = ((s8[9437184]{0:T(1024)(128)(4,1)}), s8[4194304]{0:T(1024)(128)(4,1)S(1)}, s32[]{:S(2)}) async-start(s8[9437184]{0:T(1024)(128)(4,1)} %bitcast.11), calls=%async_computation.2 | async-start | bytes 8388608
  41.4 5.4 %slice-start.1 = ((s8[9437184]{0:T(1024)(128)(4,1)}), s8[4194304]{0:T(1024)(128)(4,1)S(1)}, s32[]{:S(2)}) async-start(s8[9437184]{0:T(1024)(128)(4,1)} %bitcast.11), calls=%async_computation.3 | async-start | bytes 8388608
  41.4 5.4 %slice-start.2 = ((s8[9437184]{0:T(1024)(128)(4,1)}), s8[1048576]{0:T(1024)(128)(4,1)S(1)}, s32[]{:S(2)}) async-start(s8[9437184]{0:T(1024)(128)(4,1)} %bitcast.11), calls=%async_computation.4 | async-start | bytes 2097152
  82.3 0.7 copy-start.2
where the time goes:
time: 84.6 us; the launch traced here: 84.4 us
  blocking collectives  65.1 us (77%)
  matrix products  12.7 us (15%)
  local copies, waits for them, and re-layouts  4.36 us (5%)
  other arithmetic  2.1 us (2%)
    all_to_all x1, blocking collectives, local(): lax.all_to_all(shaped, ('ex', 'ey'), split_axis=1, concat_axis=1, tiled=T...  36.2 us
    all_to_all x1, blocking collectives, local(): lax.all_to_all(shaped_back, ('ex', 'ey'), split_axis=1, concat_axis=1, ti...  28.9 us
    dot_general x1, matrix products, local(): jnp.einsum('lrd,ldf->lrf', batch, weight_in, preferred_element_type=jnp.f...  5.32 us
    dot_general x1, matrix products, local(): jnp.einsum('lrf,lfd->lrd', hidden, weight_out, preferred_element_type=jnp...  5.1 us

commit v1 on v0

v1 whole, which is shorter than its diff:
```python
import jax
import jax.numpy as jnp
from jax import lax
from jax.experimental import pallas as pl
from jax.experimental.pallas import tpu as pltpu
from jax.sharding import PartitionSpec as P

MESH = pl.DeviceIdType.MESH
NZ, NY, NX, NC = 4, 4, 4, 2
CAP = 4
CHUNKS = 4
PER = NY * NX * NC
BF, F32 = jnp.bfloat16, jnp.float32


def position():
    e, q = lax.axis_index("ex"), lax.axis_index("ey")
    return lax.div(e, NY), lax.rem(e, NY), lax.div(q, NC), lax.rem(q, NC)


def peers(chunk, sign, visit):
    z, y, x, c = position()

    def rows(dy, carry):
        yy = lax.rem(y + NY + sign * dy, NY)
        for dx in range(NX):
            dz = lax.rem(chunk + 2 * NZ - dy - dx, NZ)
            zz = lax.rem(z + NZ + sign * dz, NZ)
            xx = lax.rem(x + NX + sign * dx, NX)
            for dc in range(NC):
                cc = lax.rem(c + dc, NC)
                visit(dy * (NX * NC) + dx * NC + dc, (zz * NY + yy, xx * NC + cc))
        return carry

    lax.fori_loop(0, NY, rows, 0)


def every(visit):
    def chunk(k, carry):
        def one(j, device):
            n = k * PER + j

            @pl.when(n != 0)
            def _():
                visit(n, device)

        peers(k, 1, one)
        return carry

    lax.fori_loop(0, CHUNKS, chunk, 0)


def iota(shape, dim):
    return lax.broadcasted_iota(jnp.int32, shape, dim)


def onehot(mask):
    return jnp.where(mask, 1.0, 0.0).astype(BF)


def kernel(
    tokens, routes, sub, win_hbm, wout_hbm, out,
    win, wout, send, recv, back, home, labels, labels_in, hidden,
    w_sem, send_sem, recv_sem, lsend_sem, lrecv_sem, bsend_sem, home_sem,
):
    half = tokens.shape[1] // 2
    n_tok = tokens.shape[0]
    z, y, x, c = position()

    barrier = pltpu.get_barrier_semaphore()
    every(
        lambda n, device: pl.semaphore_signal(
            barrier, inc=1, device_id=device, device_id_type=MESH
        )
    )
    loads = []
    for e in range(win.shape[0]):
        loads.append(pltpu.make_async_copy(win_hbm.at[e], win.at[e], w_sem.at[2 * e]))
        loads.append(pltpu.make_async_copy(wout_hbm.at[e], wout.at[e], w_sem.at[2 * e + 1]))
    for load in loads:
        load.start()

    owner = routes[...]
    oz, oy = owner // (NY * NX * NC), (owner // (NX * NC)) % NY
    ox, oc = (owner // NC) % NX, owner % NC
    dz, dy = (oz + NZ - z) % NZ, (oy + NY - y) % NY
    dx, dc = (ox + NX - x) % NX, (oc + NC - c) % NC
    number = ((dz + dy + dx) % CHUNKS) * PER + dy * (NX * NC) + dx * NC + dc
    row, lane = iota((n_tok, n_tok), 0), iota((n_tok, n_tok), 1)
    diagonal = row == lane
    number_row = number.astype(F32)
    sub_row = sub[...].astype(F32)
    number_col = jnp.sum(jnp.where(diagonal, number_row, 0.0), axis=1, keepdims=True)
    sub_col = jnp.sum(jnp.where(diagonal, sub_row, 0.0), axis=1, keepdims=True)
    same = jnp.where(number_col == number_row, 1.0, 0.0)
    slot_row = jnp.sum(jnp.where(row < lane, same, 0.0), axis=0, keepdims=True)
    slot_col = jnp.sum(jnp.where(lane < row, same, 0.0), axis=1, keepdims=True)
    target_row = (number_row * (2 * CAP) + slot_row).astype(jnp.int32)
    target_col = (number_col * (2 * CAP) + slot_col).astype(jnp.int32)

    peer = iota((CHUNKS * PER, n_tok), 0).astype(F32)
    lanes = iota((n_tok, 128), 1).astype(F32)
    chosen = jnp.where(slot_col == lanes, sub_col, 0.0).astype(BF)
    labels[...] = (
        jnp.dot(onehot(peer == number_row), chosen, preferred_element_type=F32)
        .astype(jnp.int32)
        .reshape(labels.shape)
    )

    rows = PER * 2 * CAP
    place_row = iota((rows, n_tok), 0)
    left, right = tokens[:, :half], tokens[:, half:]

    def place(k, carry):
        at = place_row + k * rows
        block = jnp.dot(onehot(at == target_row), left, preferred_element_type=F32)
        block += jnp.dot(onehot(at == target_row + CAP), right, preferred_element_type=F32)
        send[pl.ds(k * PER, PER)] = block.astype(BF).reshape(PER, 2 * CAP, half)
        return carry

    lax.fori_loop(0, CHUNKS, place, 0)

    pl.semaphore_wait(barrier, CHUNKS * PER - 1)

    def dispatch(k, carry):
        def one(j, device):
            n = k * PER + j

            def remote():
                pltpu.make_async_remote_copy(
                    labels.at[n], labels_in.at[n], lsend_sem, lrecv_sem.at[k],
                    device_id=device, device_id_type=MESH,
                ).start()
                pltpu.make_async_remote_copy(
                    send.at[n], recv.at[n], send_sem, recv_sem.at[k],
                    device_id=device, device_id_type=MESH,
                ).start()

            pl.when(n != 0)(remote)

        peers(k, 1, one)
        return carry

    pltpu.make_async_copy(labels.at[0], labels_in.at[0], lrecv_sem.at[0]).start()
    pltpu.make_async_copy(send.at[0], recv.at[0], recv_sem.at[0]).start()
    lax.fori_loop(0, CHUNKS, dispatch, 0)

    for load in loads:
        load.wait()

    m = PER * CAP
    to, fro = iota((rows, rows), 0), iota((rows, rows), 1)

    def origin(r):
        h, p = r // m, r % m
        return (p // CAP) * (2 * CAP) + h * CAP + p % CAP

    split = onehot(fro == origin(to))
    join = onehot(to == origin(fro))
    spread = onehot(iota((m, PER), 0) // CAP == iota((m, PER), 1))
    own_lane = iota((m, 128), 0) % CAP == iota((m, 128), 1)

    def compute(k, carry):
        mine = pl.ds(k * PER, PER)
        pltpu.make_async_copy(labels.at[mine], labels_in.at[mine], lrecv_sem.at[k]).wait()
        pltpu.make_async_copy(send.at[mine], recv.at[mine], recv_sem.at[k]).wait()
        label = jnp.dot(
            spread,
            labels_in[mine].reshape(PER, 128).astype(F32).astype(BF),
            preferred_element_type=F32,
        )
        label = jnp.sum(jnp.where(own_lane, label, 0.0), axis=1, keepdims=True)
        arrived = recv[mine].reshape(rows, half)
        halves = jnp.dot(split, arrived, preferred_element_type=F32)
        batch = jnp.concatenate([halves[:m], halves[m:]], axis=1)
        total = None
        for e in range(win.shape[0]):
            part = jnp.where(label == e, batch, 0.0).astype(BF)
            hidden[...] = jnp.maximum(
                jnp.dot(part, win[e], preferred_element_type=F32), 0.0
            ).astype(BF)
            result = jnp.dot(hidden[...], wout[e], preferred_element_type=F32)
            total = result if total is None else total + result
        total = total.astype(BF)
        stacked = jnp.concatenate([total[:, :half], total[:, half:]], axis=0)
        block = jnp.dot(join, stacked, preferred_element_type=F32).astype(BF)
        back[mine] = block.reshape(PER, 2 * CAP, half)

        def one(j, device):
            n = k * PER + j

            @pl.when(n != 0)
            def _():
                pltpu.make_async_remote_copy(
                    back.at[n], home.at[n], bsend_sem, home_sem.at[k],
                    device_id=device, device_id_type=MESH,
                ).start()


        peers(k, -1, one)

        @pl.when(k == 0)
        def _():
            pltpu.make_async_copy(back.at[0], home.at[0], home_sem.at[0]).start()

        return carry

    lax.fori_loop(0, CHUNKS, compute, 0)

    take_lane = iota((n_tok, rows), 1)
    out_left = out_right = None
    for k in range(CHUNKS):
        mine = pl.ds(k * PER, PER)
        at = take_lane + k * rows
        take_left = onehot(at == target_col)
        take_right = onehot(at == target_col + CAP)
        pltpu.make_async_copy(back.at[mine], home.at[mine], home_sem.at[k]).wait()
        returned = home[mine].reshape(rows, half)
        a = jnp.dot(take_left, returned, preferred_element_type=F32)
        b = jnp.dot(take_right, returned, preferred_element_type=F32)
        out_left = a if k == 0 else out_left + a
        out_right = b if k == 0 else out_right + b
    out[:, :half] = out_left.astype(BF)
    out[:, half:] = out_right.astype(BF)

    others = pl.ds(1, CHUNKS * PER - 1)
    pltpu.make_async_copy(labels.at[others], labels_in.at[others], lsend_sem).wait()
    pltpu.make_async_copy(send.at[others], recv.at[others], send_sem).wait()
    pltpu.make_async_copy(back.at[others], home.at[others], bsend_sem).wait()


def local(tokens, routes, sub_expert, probability, weight_in, weight_out):
    n_tok, width = tokens.shape
    experts, _, units = weight_in.shape
    n = CHUNKS * PER
    vmem, hbm = pl.BlockSpec(memory_space=pltpu.VMEM), pl.BlockSpec(memory_space=pl.ANY)
    blocks = pltpu.VMEM((n, 2 * CAP, width // 2), BF)
    dma = pltpu.SemaphoreType.DMA
    gathered = pl.pallas_call(
        kernel,
        out_shape=jax.ShapeDtypeStruct((n_tok, width), BF),
        in_specs=[vmem, vmem, vmem, hbm, hbm],
        out_specs=vmem,
        scratch_shapes=[
            pltpu.VMEM(weight_in.shape, BF),
            pltpu.VMEM(weight_out.shape, BF),
            blocks, blocks, blocks, blocks,
            pltpu.VMEM((n, 1, 128), jnp.int32),
            pltpu.VMEM((n, 1, 128), jnp.int32),
            pltpu.VMEM((PER * CAP, units), BF),
            dma((2 * experts,)), dma, dma((CHUNKS,)), dma, dma((CHUNKS,)), dma, dma((CHUNKS,)),
        ],
        compiler_params=pltpu.CompilerParams(
            collective_id=0, has_side_effects=True, vmem_limit_bytes=48 << 20
        ),
    )(tokens, routes.reshape(1, n_tok), sub_expert.reshape(1, n_tok), weight_in, weight_out)
    return (gathered.astype(F32) * probability[:, None]).astype(BF)


def solution(mesh):
    return jax.shard_map(
        local,
        mesh=mesh,
        in_specs=(
            P(("ex", "ey"), None),
            P(("ex", "ey"), None),
            P(("ex", "ey")),
            P(("ex", "ey")),
            P(("ex", "ey"), None, None),
            P(("ex", "ey"), None, None),
        ),
        out_specs=P(("ex", "ey"), None),
        check_vma=False,
    )
```

time: 84.6 us -> 43.7 us (0.52)
  blocking collectives: 65.1 us -> 0 us
  Pallas kernels: 0 us -> 40.3 us
  matrix products: 12.7 us -> 0 us
  local copies, waits for them, and re-layouts: 4.36 us -> 2.36 us
  other arithmetic: 2.1 us -> 0.88 us
    all_to_all x2 -> x0, blocking collectives: 65.1 us -> none  [the longest x1 36.2 us: local(): lax.all_to_all(shaped, ('ex', 'ey'), split_axis=1, concat_axis=1, tiled=T...]
    pallas_call x0 -> x1, Pallas kernels: none -> 40.3 us  [local(): pl.pallas_call(kernel, out_shape=jax.ShapeDtypeStruct((n_tok, width), BF)...]
    dot_general x5 -> x0, matrix products: 12.7 us -> none  [the longest x1 5.32 us: local(): jnp.einsum('lrd,ldf->lrf', batch, weight_in, preferred_element_type=jnp.f...]
    reshape x5 -> x0, local copies, waits for them, and re-layouts: 2.28 us -> none  [the longest x2 0.94 us: local(): shaped = outgoing.reshape(local_experts, devices_all, capacity, width)]
    unnamed x12 -> x8, local copies, waits for them, and re-layouts: 0.3 us -> 2.36 us
    all_to_all x2 -> x0, local copies, waits for them, and re-layouts: 1.78 us -> none  [the longest x1 1.24 us: local(): lax.all_to_all(shaped, ('ex', 'ey'), split_axis=1, concat_axis=1, tiled=T...]
    add x2 -> x0, other arithmetic: 1.37 us -> none  [the longest x1 0.69 us: local(): target = sub_expert * (devices_all * capacity) + owner * capacity + slot]
    convert_element_type x0 -> x1, other arithmetic: none -> 0.88 us  [local(): return (gathered.astype(F32) * probability[:, None]).astype(BF)]
where the time goes in v1:
time: 43.7 us; the launch traced here: 43.5 us
  Pallas kernels  40.3 us (92%)
  local copies, waits for them, and re-layouts  2.36 us (5%)
  other arithmetic  0.88 us (2%)
    pallas_call x1, Pallas kernels, local(): pl.pallas_call(kernel, out_shape=jax.ShapeDtypeStruct((n_tok, width), BF)...  40.3 us
    unnamed x8, local copies, waits for them, and re-layouts  2.36 us
    convert_element_type x1, other arithmetic, local(): return (gathered.astype(F32) * probability[:, None]).astype(BF)  0.88 us

profile of v1, /device:TPU:1, one launch (start us, length us, event | category | flops | bytes accessed | tf_op | source)
XLA Modules:
  0.0 43.5 jit_solution(2553938202820081762)
XLA Ops:
  0.0 0.0 copy-start
  0.0 1.0 %copy-done = bf16[256,768]{1,0:T(8,128)(2,1)S(1)} copy-done((bf16[256,768]{1,0:T(8,128)(2,1)S(1)}, bf16[256,768]{1,0:T(8,128)(2,1)}, u32[]{:S(2)}) %copy-start) | copy-done | bytes 393240
  1.0 0.0 copy-start.1
  1.0 0.7 %copy-done.1 = s32[256,1]{0,1:T(1,128)S(1)} copy-done((s32[256,1]{0,1:T(1,128)S(1)}, s32[256,1]{0,1:T(1,128)}, u32[]{:S(2)}) %copy-start.1) | copy-done | bytes 1048
  1.7 0.0 copy-start.2
  1.7 0.7 %copy-done.2 = s32[256]{0:T(256)S(1)} copy-done((s32[256]{0:T(256)S(1)}, s32[256]{0:T(256)}, u32[]{:S(2)}) %copy-start.2) | copy-done | bytes 1048
  2.4 0.0 copy-start.3
  2.4 40.3 %shard_map.64 = bf16[256,768]{1,0:T(8,128)(2,1)S(1)} custom-call(bf16[256,768]{1,0:T(8,128)(2,1)S(1)} %copy-done, s32[1,256]{1,0:T(1,128)S(1)} %bitcast.2, s32[1,256]{1,0:T(1,128)S(1)} %bitcast.3, bf16[2,768,3072]{2,1,0:T(8,128)(2,1)} %win_hbm.1, bf16[2,3072,768]{2,1,0:T(8,128)(2,1)} %wout_hbm.1), custom_call_target="tpu_custom_call" | custom-call | tf_op jit(solution)/shard_map/pallas_call | solution.py:239
  42.7 0.0 copy-done.3
  42.7 0.9 %multiply_convert_fusion = bf16[256,768]{1,0:T(8,128)(2,1)} fusion(bf16[256,768]{1,0:T(8,128)(2,1)S(1)} %shard_map.64, f32[256]{0:T(256)S(1)} %copy-done.3), kind=kLoop, calls=%fused_computation | loop fusion | flops 589824 | bytes 787456 | tf_op jit(solution)/shard_map/convert_element_type | solution.py:257
Async XLA Ops:
  0.0 1.0 %copy-start = (bf16[256,768]{1,0:T(8,128)(2,1)S(1)}, bf16[256,768]{1,0:T(8,128)(2,1)}, u32[]{:S(2)}) copy-start(bf16[256,768]{1,0:T(8,128)(2,1)} %tokens.1) | copy-start | bytes 1179652
  1.0 0.7 %copy-start.1 = (s32[256,1]{0,1:T(1,128)S(1)}, s32[256,1]{0,1:T(1,128)}, u32[]{:S(2)}) copy-start(s32[256,1]{0,1:T(1,128)} %param.7) | copy-start | bytes 3076
  1.7 0.7 %copy-start.2 = (s32[256]{0:T(256)S(1)}, s32[256]{0:T(256)}, u32[]{:S(2)}) copy-start(s32[256]{0:T(256)} %param.8) | copy-start | bytes 3076
  2.4 40.3 %copy-start.3 = (f32[256]{0:T(256)S(1)}, f32[256]{0:T(256)}, u32[]{:S(2)}) copy-start(f32[256]{0:T(256)} %param.9) | copy-start | bytes 3076

commit v2 on v1

v2 whole, which is shorter than its diff:
```python
import jax
import jax.numpy as jnp
from jax import lax
from jax.experimental import pallas as pl
from jax.experimental.pallas import tpu as pltpu
from jax.sharding import PartitionSpec as P

MESH = pl.DeviceIdType.MESH
NZ, NY, NX, NC = 4, 4, 4, 2
CAP = 4
CHUNKS = 4
PER = NZ * NY * NX * NC // CHUNKS
BF, F32 = jnp.bfloat16, jnp.float32


def chip_order():
    chips = [(a, b, c) for a in range(NZ) for b in range(NY) for c in range(NX)]

    def kind(o):
        return "".join(str(d) for d in sorted((min(d, 4 - d) for d in o), reverse=True))

    def group(name, parity=None):
        found = [o for o in chips if kind(o) == name]
        if parity is None:
            return found
        return [o for o in found if sum(d == 3 for d in o) % 2 == parity]

    bent = group("210")
    near = group("000") + group("100") + group("200") + group("110", 0)
    second = group("110", 1) + group("111") + [bent[0], bent[-1]]
    middle = bent[1:-1] + group("211", 0)
    far = group("211", 1) + group("220") + group("221") + group("222")
    return near + middle + far + second


ORDER = chip_order()
SIDE = len(ORDER) // CHUNKS


def position():
    e, q = lax.axis_index("ex"), lax.axis_index("ey")
    return lax.div(e, NY), lax.rem(e, NY), lax.div(q, NC), lax.rem(q, NC)


def peers(chunk, sign, visit):
    z, y, x, c = position()
    flags = [jnp.where(chunk == k, 1, 0) for k in range(1, CHUNKS)]

    def offset(i, axis):
        values = [ORDER[k * SIDE + i][axis] for k in range(CHUNKS)]
        total = values[0]
        for flag, value in zip(flags, values[1:]):
            if value != values[0]:
                total = total + flag * (value - values[0])
        return total

    for i in reversed(range(SIDE)):
        dz, dy, dx = (offset(i, axis) for axis in range(3))
        zz = lax.rem(z + NZ + sign * dz, NZ)
        yy = lax.rem(y + NY + sign * dy, NY)
        xx = lax.rem(x + NX + sign * dx, NX)
        for dc in reversed(range(NC)):
            device = (zz * NY + yy, xx * NC + lax.rem(c + dc, NC))
            n = chunk * PER + i * NC + dc
            if i + dc == 0:
                pl.when(n != 0)(lambda n=n, device=device: visit(n, device))
            else:
                visit(n, device)


def iota(shape, dim):
    return lax.broadcasted_iota(jnp.int32, shape, dim)


def onehot(mask):
    return jnp.where(mask, 1.0, 0.0).astype(BF)


def push(src, dst, send_sem, recv_sem, device):
    pltpu.make_async_remote_copy(
        src, dst, send_sem, recv_sem, device_id=device, device_id_type=MESH
    ).start()


def kernel(
    tokens_hbm, routes_hbm, sub_hbm, win_hbm, wout_hbm, out,
    tokens, routes, sub, win, wout, send, recv, back, home, labels, labels_in, hidden,
    in_sem, w_sem, send_sem, recv_sem, lsend_sem, lrecv_sem, bsend_sem, home_sem,
):
    n_tok, half = tokens.shape[0], tokens.shape[1] // 2
    z, y, x, c = position()

    barrier = pltpu.get_barrier_semaphore()

    def greet(i, carry):
        peers(
            lax.rem(CHUNKS + 2 - i, CHUNKS),
            1,
            lambda n, device: pl.semaphore_signal(
                barrier, inc=1, device_id=device, device_id_type=MESH
            ),
        )
        return carry

    lax.fori_loop(0, CHUNKS, greet, 0)
    small = [
        pltpu.make_async_copy(src, dst, in_sem.at[i])
        for i, (src, dst) in enumerate(
            ((routes_hbm, routes), (sub_hbm, sub), (tokens_hbm, tokens))
        )
    ]
    loads = []
    for e in range(win.shape[0]):
        loads.append(pltpu.make_async_copy(win_hbm.at[e], win.at[e], w_sem.at[2 * e]))
        loads.append(pltpu.make_async_copy(wout_hbm.at[e], wout.at[e], w_sem.at[2 * e + 1]))
    for load in small:
        load.start()
    for load in small:
        load.wait()
    for load in loads:
        load.start()

    owner = routes[...]
    dz = ((owner >> 5) + (NZ - z)) & (NZ - 1)
    dy = ((owner >> 3) + (NY - y)) & (NY - 1)
    dx = ((owner >> 1) + (NX - x)) & (NX - 1)
    dc = (owner + (NC - c)) & (NC - 1)
    chip = dz * (NY * NX) + dy * NX + dx
    rank = jnp.zeros_like(chip)
    for i, (a, b, d) in enumerate(ORDER):
        rank = jnp.where(chip == a * (NY * NX) + b * NX + d, i, rank)
    number = rank * NC + dc
    row, lane = iota((n_tok, n_tok), 0), iota((n_tok, n_tok), 1)
    diagonal = row == lane
    number_row = number.astype(F32)
    sub_row = sub[...].astype(F32)
    number_col = jnp.sum(jnp.where(diagonal, number_row, 0.0), axis=1, keepdims=True)
    sub_col = jnp.sum(jnp.where(diagonal, sub_row, 0.0), axis=1, keepdims=True)
    same = jnp.where(number_col == number_row, 1.0, 0.0)
    slot_row = jnp.sum(jnp.where(row < lane, same, 0.0), axis=0, keepdims=True)
    slot_col = jnp.sum(jnp.where(lane < row, same, 0.0), axis=1, keepdims=True)
    target_row = (number_row * (2 * CAP) + slot_row).astype(jnp.int32)
    target_col = (number_col * (2 * CAP) + slot_col).astype(jnp.int32)

    peer = iota((CHUNKS * PER, n_tok), 0).astype(F32)
    lanes = iota((n_tok, 128), 1).astype(F32)
    chosen = jnp.where(slot_col == lanes, sub_col, 0.0).astype(BF)
    labels[...] = (
        jnp.dot(onehot(peer == number_row), chosen, preferred_element_type=F32)
        .astype(jnp.int32)
        .reshape(labels.shape)
    )

    rows = PER * 2 * CAP
    place_row = iota((rows, n_tok), 0)

    def place(k, carry):
        at = place_row + k * rows
        block = jnp.dot(
            onehot(at == target_row), tokens[:, :half], preferred_element_type=F32
        )
        block += jnp.dot(
            onehot(at == target_row + CAP), tokens[:, half:], preferred_element_type=F32
        )
        send[pl.ds(k * PER, PER)] = block.astype(BF).reshape(PER, 2 * CAP, half)
        return carry

    lax.fori_loop(0, CHUNKS, place, 0)

    pl.semaphore_wait(barrier, CHUNKS * PER - 1)

    pltpu.make_async_copy(labels.at[0], labels_in.at[0], lrecv_sem.at[0]).start()
    pltpu.make_async_copy(send.at[0], recv.at[0], recv_sem.at[0]).start()

    def dispatch(k, carry):
        def visit(n, device):
            push(labels.at[n], labels_in.at[n], lsend_sem, lrecv_sem.at[k], device)
            push(send.at[n], recv.at[n], send_sem, recv_sem.at[k], device)

        peers(k, 1, visit)
        return carry

    lax.fori_loop(0, CHUNKS, dispatch, 0)

    m = PER * CAP
    to, fro = iota((rows, rows), 0), iota((rows, rows), 1)

    def origin(r):
        return ((r & (m - 1)) >> 2) * (2 * CAP) + (r >> 7) * CAP + (r & (CAP - 1))

    split = onehot(fro == origin(to))
    join = onehot(to == origin(fro))
    spread = onehot((iota((m, PER), 0) >> 2) == iota((m, PER), 1))
    own_lane = (iota((m, 128), 0) & (CAP - 1)) == iota((m, 128), 1)

    for load in loads:
        load.wait()

    def compute(k, carry):
        mine = pl.ds(k * PER, PER)
        pltpu.make_async_copy(labels.at[mine], labels_in.at[mine], lrecv_sem.at[k]).wait()
        label = jnp.dot(
            spread,
            labels_in[mine].reshape(PER, 128).astype(F32).astype(BF),
            preferred_element_type=F32,
        )
        label = jnp.sum(jnp.where(own_lane, label, 0.0), axis=1, keepdims=True)
        pltpu.make_async_copy(send.at[mine], recv.at[mine], recv_sem.at[k]).wait()
        arrived = recv[mine].reshape(rows, half)
        halves = jnp.dot(split, arrived, preferred_element_type=F32)
        batch = jnp.concatenate([halves[:m], halves[m:]], axis=1)
        total = None
        for e in range(win.shape[0]):
            part = jnp.where(label == e, batch, 0.0).astype(BF)
            hidden[...] = jnp.maximum(
                jnp.dot(part, win[e], preferred_element_type=F32), 0.0
            ).astype(BF)
            result = jnp.dot(hidden[...], wout[e], preferred_element_type=F32)
            total = result if total is None else total + result
        total = total.astype(BF)
        stacked = jnp.concatenate([total[:, :half], total[:, half:]], axis=0)
        block = jnp.dot(join, stacked, preferred_element_type=F32).astype(BF)
        back[mine] = block.reshape(PER, 2 * CAP, half)

        @pl.when(k == 0)
        def _():
            pltpu.make_async_copy(back.at[0], home.at[0], home_sem.at[0]).start()

        peers(
            k,
            -1,
            lambda n, device: push(back.at[n], home.at[n], bsend_sem, home_sem.at[k], device),
        )
        return carry

    lax.fori_loop(0, CHUNKS, compute, 0)

    take_lane = iota((n_tok, rows), 1)
    out_left = out_right = None
    for k in range(CHUNKS):
        mine = pl.ds(k * PER, PER)
        at = take_lane + k * rows
        take_left = onehot(at == target_col)
        take_right = onehot(at == target_col + CAP)
        pltpu.make_async_copy(back.at[mine], home.at[mine], home_sem.at[k]).wait()
        returned = home[mine].reshape(rows, half)
        a = jnp.dot(take_left, returned, preferred_element_type=F32)
        b = jnp.dot(take_right, returned, preferred_element_type=F32)
        out_left = a if k == 0 else out_left + a
        out_right = b if k == 0 else out_right + b
    out[:, :half] = out_left.astype(BF)
    out[:, half:] = out_right.astype(BF)

    others = pl.ds(1, CHUNKS * PER - 1)
    pltpu.make_async_copy(labels.at[others], labels_in.at[others], lsend_sem).wait()
    pltpu.make_async_copy(send.at[others], recv.at[others], send_sem).wait()
    pltpu.make_async_copy(back.at[others], home.at[others], bsend_sem).wait()


def local(tokens, routes, sub_expert, probability, weight_in, weight_out):
    n_tok, width = tokens.shape
    experts, _, units = weight_in.shape
    n = CHUNKS * PER
    blocks = pltpu.VMEM((n, 2 * CAP, width // 2), BF)
    dma = pltpu.SemaphoreType.DMA
    gathered = pl.pallas_call(
        kernel,
        out_shape=jax.ShapeDtypeStruct((n_tok, width), BF),
        in_specs=[pl.BlockSpec(memory_space=pltpu.MemorySpace.HBM)] * 5,
        out_specs=pl.BlockSpec(memory_space=pltpu.VMEM),
        scratch_shapes=[
            pltpu.VMEM((n_tok, width), BF),
            pltpu.VMEM((1, n_tok), jnp.int32),
            pltpu.VMEM((1, n_tok), jnp.int32),
            pltpu.VMEM(weight_in.shape, BF),
            pltpu.VMEM(weight_out.shape, BF),
            blocks, blocks, blocks, blocks,
            pltpu.VMEM((n, 1, 128), jnp.int32),
            pltpu.VMEM((n, 1, 128), jnp.int32),
            pltpu.VMEM((PER * CAP, units), BF),
            dma((3,)), dma((2 * experts,)),
            dma, dma((CHUNKS,)), dma, dma((CHUNKS,)), dma, dma((CHUNKS,)),
        ],
        compiler_params=pltpu.CompilerParams(
            collective_id=0, has_side_effects=True, vmem_limit_bytes=56000000
        ),
    )(tokens, routes.reshape(1, n_tok), sub_expert.reshape(1, n_tok), weight_in, weight_out)
    return (gathered.astype(F32) * probability[:, None]).astype(BF)


def solution(mesh):
    return jax.shard_map(
        local,
        mesh=mesh,
        in_specs=(
            P(("ex", "ey"), None),
            P(("ex", "ey"), None),
            P(("ex", "ey")),
            P(("ex", "ey")),
            P(("ex", "ey"), None, None),
            P(("ex", "ey"), None, None),
        ),
        out_specs=P(("ex", "ey"), None),
        check_vma=False,
    )
```

time: 43.7 us -> 40.3 us (0.922)
  the two profiles are of different devices: /device:TPU:1 before, /device:TPU:6 now
where the time goes in v2:
time: 40.3 us; the launch traced here: 40.1 us
  Pallas kernels  37.9 us (94%)
  local copies, waits for them, and re-layouts  1.36 us (3%)
  other arithmetic  0.88 us (2%)
    pallas_call x1, Pallas kernels, local(): pl.pallas_call(kernel, out_shape=jax.ShapeDtypeStruct((n_tok, width), BF)...  37.9 us
    unnamed x6, local copies, waits for them, and re-layouts  1.36 us
    convert_element_type x1, other arithmetic, local(): return (gathered.astype(F32) * probability[:, None]).astype(BF)  0.88 us

profile of v2, /device:TPU:6, one launch (start us, length us, event | category | flops | bytes accessed | tf_op | source)
XLA Modules:
  0.0 40.1 jit_solution(6020298754957630292)
XLA Ops:
  0.0 0.0 copy-start
  0.0 0.7 %copy-done = s32[256,1]{0,1:T(1,128)S(1)} copy-done((s32[256,1]{0,1:T(1,128)S(1)}, s32[256,1]{0,1:T(1,128)}, u32[]{:S(2)}) %copy-start) | copy-done | bytes 1048
  0.7 0.0 copy-start.1
  0.7 0.7 %copy-done.1 = s32[256]{0:T(256)S(1)} copy-done((s32[256]{0:T(256)S(1)}, s32[256]{0:T(256)}, u32[]{:S(2)}) %copy-start.1) | copy-done | bytes 1048
  1.4 0.0 copy-start.2
  1.4 37.9 %shard_map.64 = bf16[256,768]{1,0:T(8,128)(2,1)S(1)} custom-call(bf16[256,768]{1,0:T(8,128)(2,1)} %tokens_hbm.1, s32[1,256]{1,0:T(1,128)S(1)} %bitcast.2, s32[1,256]{1,0:T(1,128)S(1)} %bitcast.3, bf16[2,768,3072]{2,1,0:T(8,128)(2,1)} %win_hbm.1, bf16[2,3072,768]{2,1,0:T(8,128)(2,1)} %wout_hbm.1), custom_call_target="tpu_custom_call" | custom-call | tf_op jit(solution)/shard_map/pallas_call | solution.py:266
  39.2 0.0 copy-done.2
  39.2 0.9 %multiply_convert_fusion = bf16[256,768]{1,0:T(8,128)(2,1)} fusion(bf16[256,768]{1,0:T(8,128)(2,1)S(1)} %shard_map.64, f32[256]{0:T(256)S(1)} %copy-done.2), kind=kLoop, calls=%fused_computation | loop fusion | flops 589824 | bytes 787456 | tf_op jit(solution)/shard_map/convert_element_type | solution.py:288
Async XLA Ops:
  0.0 0.7 %copy-start = (s32[256,1]{0,1:T(1,128)S(1)}, s32[256,1]{0,1:T(1,128)}, u32[]{:S(2)}) copy-start(s32[256,1]{0,1:T(1,128)} %param.7) | copy-start | bytes 3076
  0.7 0.7 %copy-start.1 = (s32[256]{0:T(256)S(1)}, s32[256]{0:T(256)}, u32[]{:S(2)}) copy-start(s32[256]{0:T(256)} %param.8) | copy-start | bytes 3076
  1.4 37.9 %copy-start.2 = (f32[256]{0:T(256)S(1)}, f32[256]{0:T(256)}, u32[]{:S(2)}) copy-start(f32[256]{0:T(256)} %param.9) | copy-start | bytes 3076

commit v3 on v2

--- a/solution.py
+++ b/solution.py
@@ -88,6 +88,7 @@
     in_sem, w_sem, send_sem, recv_sem, lsend_sem, lrecv_sem, bsend_sem, home_sem,
 ):
     n_tok, half = tokens.shape[0], tokens.shape[1] // 2
+    units = win.shape[2]
     z, y, x, c = position()
 
     barrier = pltpu.get_barrier_semaphore()
@@ -112,7 +113,9 @@
     loads = []
     for e in range(win.shape[0]):
         loads.append(pltpu.make_async_copy(win_hbm.at[e], win.at[e], w_sem.at[2 * e]))
-        loads.append(pltpu.make_async_copy(wout_hbm.at[e], wout.at[e], w_sem.at[2 * e + 1]))
+        loads.append(pltpu.make_async_copy(
+            wout_hbm.at[e], wout.at[pl.ds(e * units, units)], w_sem.at[2 * e + 1]
+        ))
     for load in small:
         load.start()
     for load in small:
@@ -209,14 +212,12 @@
         arrived = recv[mine].reshape(rows, half)
         halves = jnp.dot(split, arrived, preferred_element_type=F32)
         batch = jnp.concatenate([halves[:m], halves[m:]], axis=1)
-        total = None
         for e in range(win.shape[0]):
             part = jnp.where(label == e, batch, 0.0).astype(BF)
-            hidden[...] = jnp.maximum(
+            hidden[:, e * units : (e + 1) * units] = jnp.maximum(
                 jnp.dot(part, win[e], preferred_element_type=F32), 0.0
             ).astype(BF)
-            result = jnp.dot(hidden[...], wout[e], preferred_element_type=F32)
-            total = result if total is None else total + result
+        total = jnp.dot(hidden[...], wout[...], preferred_element_type=F32)
         total = total.astype(BF)
         stacked = jnp.concatenate([total[:, :half], total[:, half:]], axis=0)
         block = jnp.dot(join, stacked, preferred_element_type=F32).astype(BF)
@@ -237,7 +238,7 @@
 
     take_lane = iota((n_tok, rows), 1)
     out_left = out_right = None
-    for k in range(CHUNKS):
+    for k in (0, 1, 3, 2):
         mine = pl.ds(k * PER, PER)
         at = take_lane + k * rows
         take_left = onehot(at == target_col)
@@ -273,11 +274,11 @@
             pltpu.VMEM((1, n_tok), jnp.int32),
             pltpu.VMEM((1, n_tok), jnp.int32),
             pltpu.VMEM(weight_in.shape, BF),
-            pltpu.VMEM(weight_out.shape, BF),
+            pltpu.VMEM((experts * units, width), BF),
             blocks, blocks, blocks, blocks,
             pltpu.VMEM((n, 1, 128), jnp.int32),
             pltpu.VMEM((n, 1, 128), jnp.int32),
-            pltpu.VMEM((PER * CAP, units), BF),
+            pltpu.VMEM((PER * CAP, experts * units), BF),
             dma((3,)), dma((2 * experts,)),
             dma, dma((CHUNKS,)), dma, dma((CHUNKS,)), dma, dma((CHUNKS,)),
         ],

time: 40.3 us -> 39.9 us (0.990)
  no operation moved by 1% of the time
where the time goes in v3:
time: 39.9 us; the launch traced here: 39.7 us
  Pallas kernels  37.5 us (94%)
  local copies, waits for them, and re-layouts  1.36 us (3%)
  other arithmetic  0.88 us (2%)
    pallas_call x1, Pallas kernels, local(): pl.pallas_call(kernel, out_shape=jax.ShapeDtypeStruct((n_tok, width), BF)...  37.5 us
    unnamed x6, local copies, waits for them, and re-layouts  1.36 us
    convert_element_type x1, other arithmetic, local(): return (gathered.astype(F32) * probability[:, None]).astype(BF)  0.88 us

profile of v3, /device:TPU:6, one launch (start us, length us, event | category | flops | bytes accessed | tf_op | source)
XLA Modules:
  0.0 39.7 jit_solution(8405227073776252158)
XLA Ops:
  0.0 0.0 copy-start
  0.0 0.7 %copy-done = s32[256,1]{0,1:T(1,128)S(1)} copy-done((s32[256,1]{0,1:T(1,128)S(1)}, s32[256,1]{0,1:T(1,128)}, u32[]{:S(2)}) %copy-start) | copy-done | bytes 1048
  0.7 0.0 copy-start.1
  0.7 0.7 %copy-done.1 = s32[256]{0:T(256)S(1)} copy-done((s32[256]{0:T(256)S(1)}, s32[256]{0:T(256)}, u32[]{:S(2)}) %copy-start.1) | copy-done | bytes 1048
  1.4 0.0 copy-start.2
  1.4 37.5 %shard_map.64 = bf16[256,768]{1,0:T(8,128)(2,1)S(1)} custom-call(bf16[256,768]{1,0:T(8,128)(2,1)} %tokens_hbm.1, s32[1,256]{1,0:T(1,128)S(1)} %bitcast.2, s32[1,256]{1,0:T(1,128)S(1)} %bitcast.3, bf16[2,768,3072]{2,1,0:T(8,128)(2,1)} %win_hbm.1, bf16[2,3072,768]{2,1,0:T(8,128)(2,1)} %wout_hbm.1), custom_call_target="tpu_custom_call" | custom-call | tf_op jit(solution)/shard_map/pallas_call | solution.py:267
  38.8 0.0 copy-done.2
  38.8 0.9 %multiply_convert_fusion = bf16[256,768]{1,0:T(8,128)(2,1)} fusion(bf16[256,768]{1,0:T(8,128)(2,1)S(1)} %shard_map.64, f32[256]{0:T(256)S(1)} %copy-done.2), kind=kLoop, calls=%fused_computation | loop fusion | flops 589824 | bytes 787456 | tf_op jit(solution)/shard_map/convert_element_type | solution.py:289
Async XLA Ops:
  0.0 0.7 %copy-start = (s32[256,1]{0,1:T(1,128)S(1)}, s32[256,1]{0,1:T(1,128)}, u32[]{:S(2)}) copy-start(s32[256,1]{0,1:T(1,128)} %param.7) | copy-start | bytes 3076
  0.7 0.7 %copy-start.1 = (s32[256]{0:T(256)S(1)}, s32[256]{0:T(256)}, u32[]{:S(2)}) copy-start(s32[256]{0:T(256)} %param.8) | copy-start | bytes 3076
  1.4 37.5 %copy-start.2 = (f32[256]{0:T(256)S(1)}, f32[256]{0:T(256)}, u32[]{:S(2)}) copy-start(f32[256]{0:T(256)} %param.9) | copy-start | bytes 3076

commit v4 on v3

--- a/solution.py
+++ b/solution.py
@@ -256,6 +256,10 @@
     pltpu.make_async_copy(labels.at[others], labels_in.at[others], lsend_sem).wait()
     pltpu.make_async_copy(send.at[others], recv.at[others], send_sem).wait()
     pltpu.make_async_copy(back.at[others], home.at[others], bsend_sem).wait()
+
+
+def pinned(operand):
+    return pltpu.with_memory_space_constraint(operand, pltpu.MemorySpace.HBM)
 
 
 def local(tokens, routes, sub_expert, probability, weight_in, weight_out):
@@ -285,7 +289,13 @@
         compiler_params=pltpu.CompilerParams(
             collective_id=0, has_side_effects=True, vmem_limit_bytes=56000000
         ),
-    )(tokens, routes.reshape(1, n_tok), sub_expert.reshape(1, n_tok), weight_in, weight_out)
+    )(
+        tokens,
+        pinned(routes.reshape(1, n_tok)),
+        pinned(sub_expert.reshape(1, n_tok)),
+        weight_in,
+        weight_out,
+    )
     return (gathered.astype(F32) * probability[:, None]).astype(BF)
 
 

time: 39.9 us -> 38.5 us (0.965)
  local copies, waits for them, and re-layouts: 1.36 us -> 0.01 us
    unnamed x6 -> x2, local copies, waits for them, and re-layouts: 1.36 us -> 0.01 us
where the time goes in v4:
time: 38.5 us; the launch traced here: 38.3 us
  Pallas kernels  37.4 us (97%)
  other arithmetic  0.88 us (2%)
    pallas_call x1, Pallas kernels, local(): pl.pallas_call(kernel, out_shape=jax.ShapeDtypeStruct((n_tok, width), BF)...  37.4 us
    convert_element_type x1, other arithmetic, local(): return (gathered.astype(F32) * probability[:, None]).astype(BF)  0.88 us

profile of v4, /device:TPU:6, one launch (start us, length us, event | category | flops | bytes accessed | tf_op | source)
XLA Modules:
  0.0 38.3 jit_solution(15460599324863428463)
XLA Ops:
  0.0 0.0 copy-start
  0.0 37.4 %shard_map.64 = bf16[256,768]{1,0:T(8,128)(2,1)S(1)} custom-call(bf16[256,768]{1,0:T(8,128)(2,1)} %tokens_hbm.1, s32[1,256]{1,0:T(1,128)} %bitcast.2, s32[1,256]{1,0:T(1,128)} %bitcast.3, bf16[2,768,3072]{2,1,0:T(8,128)(2,1)} %win_hbm.1, bf16[2,3072,768]{2,1,0:T(8,128)(2,1)} %wout_hbm.1), custom_call_target="tpu_custom_call" | custom-call | tf_op jit(solution)/shard_map/pallas_call | solution.py:271
  37.5 0.0 copy-done
  37.5 0.9 %multiply_convert_fusion = bf16[256,768]{1,0:T(8,128)(2,1)} fusion(bf16[256,768]{1,0:T(8,128)(2,1)S(1)} %shard_map.64, f32[256]{0:T(256)S(1)} %copy-done), kind=kLoop, calls=%fused_computation | loop fusion | flops 589824 | bytes 787456 | tf_op jit(solution)/shard_map/convert_element_type | solution.py:299
Async XLA Ops:
  0.0 37.5 %copy-start = (f32[256]{0:T(256)S(1)}, f32[256]{0:T(256)}, u32[]{:S(2)}) copy-start(f32[256]{0:T(256)} %param.9) | copy-start | bytes 3076
